TPU v7x, 32 devices: a whole 2x2x4 slice. The times are simulated.
32 devices in a mesh: wide: 16 (over z, x, core), narrow: 2 (over y).
Axes of the slice: x: 2, y: 2, z: 4, core: 2. Of those that a mesh axis runs over, the one named last changes fastest.
Arguments:
- amplitudes: float32 [48, 1024, 1024], P('wide', None, 'narrow'), may hold values from -24 to 24
- integrals: float32 [16, 16, 1024, 1024], P('narrow', None, 'wide'), may hold values from -0.005859375 to 0.005859375
- pair_index: int32 [48, 2], P('wide'), may hold values from 0 to 199
- window_virtuals: int32 [16], replicated, may hold values from 0 to 1023
- occ_energy: float32 [200], replicated, may hold values from -3 to -0.5
- virt_energy: float32 [1024], replicated, may hold values from 0.3 to 6
Outputs:
- update: float32 [16, 16, 48], P('narrow', None, 'wide')
All inputs are finite; a program needn't handle non-finite values.
Results may differ from a plain program's by a relative error of at most 0.00013.
Values sent between devices are 32-bit elements; how exact they have to be, the bound alone decides.
No kernel may reach another device: no remote copies, remote signals or barrier semaphores. Data moves between devices by JAX's collectives and lax.ppermute only.
A program may use at most 128 MiB of HBM per device.

v0:
```python
import jax
import jax.numpy as jnp
from jax import lax
from jax.sharding import PartitionSpec as P


def lookup(table, indices):
    matches = (indices[..., None] == jnp.arange(table.shape[0], dtype=jnp.int32)).astype(
        jnp.float32
    )
    return jnp.sum(matches * table, axis=-1)


def contract(left_rows, right_rows):
    return lax.dot_general(
        left_rows.reshape(left_rows.shape[0], -1),
        right_rows.reshape(right_rows.shape[0], -1),
        (((1,), (1,)), ((), ())),
        precision=lax.Precision.HIGHEST,
        preferred_element_type=jnp.float32,
    )


def shards(amplitudes, integrals, pair_index, window_virtuals, occ_energy, virt_energy):
    exchanged = lax.all_to_all(amplitudes, "wide", split_axis=1, concat_axis=0, tiled=True)
    rows_here = integrals.shape[0]
    window = integrals.shape[1]
    first_block = integrals.shape[2]
    all_pairs = exchanged.shape[0]
    integral_rows = integrals.reshape(rows_here * window, first_block, integrals.shape[3])
    partial_value = contract(integral_rows, lax.all_gather(exchanged, "narrow", axis=2, tiled=True))
    ladder = lax.psum_scatter(
        partial_value.reshape(rows_here, window, all_pairs), "wide", scatter_dimension=2, tiled=True
    )
    swapped = lax.all_to_all(ladder, "narrow", split_axis=1, concat_axis=0, tiled=True)
    combined = ladder + jnp.transpose(swapped, (1, 0, 2))
    row_start = lax.axis_index("narrow") * rows_here
    own_virtuals = lax.dynamic_slice_in_dim(window_virtuals, row_start, rows_here, 0)
    row_energy = lookup(virt_energy, own_virtuals)
    column_energy = lookup(virt_energy, window_virtuals)
    pair_energy = lookup(occ_energy, pair_index[:, 0]) + lookup(occ_energy, pair_index[:, 1])
    denominator = (
        pair_energy[None, None, :] - row_energy[:, None, None] - column_energy[None, :, None]
    )
    return combined / denominator


def solution(mesh):
    in_specs = (
        P("wide", None, "narrow"),
        P("narrow", None, "wide", None),
        P("wide", None),
        P(),
        P(),
        P(),
    )
    out_specs = P("narrow", None, "wide")
    return jax.shard_map(shards, mesh=mesh, in_specs=in_specs, out_specs=out_specs, check_vma=False)
```

profile of v0, /device:TPU:0, one launch (start us, length us, event | category | flops | bytes accessed | tf_op | source)
XLA Modules:
  0.0 489.2 jit_solution(3291001078130395045)
XLA Ops:
  6.5 7.1 %copy.42 = f32[3,1024,512]{2,0,1:T(4,128)S(1)} copy(f32[3,1024,512]{2,1,0:T(8,128)} %param.6) | data formatting | bytes 12582912 | tf_op args[0]
  13.6 189.3 %all_to_all.36 = f32[3,1024,512]{2,0,1:T(4,128)S(1)} all-to-all(f32[3,1024,512]{2,0,1:T(4,128)S(1)} %copy.42), channel_id=1, replica_groups=mesh['wide'=16,'narrow'=2] {'wide'}, dimensions={1} | all-to-all | bytes 12582912 | tf_op jit(solution)/shard_map/all_to_all | solution.py:25
  202.9 2.0 copy.43
  205.0 1.2 copy.44
  206.2 0.0 copy-start.3
  206.2 0.0 copy-start.2
  206.2 0.0 copy-start.1
  206.2 0.0 copy-start
  206.3 6.3 %copy.45 = f32[48,64,512]{2,0,1:T(8,128)} copy(f32[48,64,512]{2,1,0:T(8,128)S(1)} %bitcast.30) | data formatting | bytes 12582912 | tf_op jit(solution)/shard_map/all_to_all | solution.py:25
  212.5 0.0 all-gather.2.cloned.1.call-update
  212.5 0.0 reduce-scatter.4.cloned.1.call-start
  212.6 0.1 dynamic_slice.3
  212.7 0.0 copy-done.2
  212.7 0.0 copy-done.1
  212.7 0.2 select_reduce_fusion.2
  212.9 0.2 select_reduce_fusion.1
  213.1 153.1 %all-gather.2.cloned.1.call-done = f32[48,64,1024]{2,0,1:T(8,128)} async-done(((f32[48,64,512]{2,0,1:T(8,128)}), f32[48,64,1024]{2,0,1:T(8,128)}) %all-gather.2.cloned.1.call-update) | async-done | bytes 12582928 | tf_op jit(solution)/shard_map/all_gather | solution.py:31
  366.2 50.3 %fusion.3 = f32[8,16,48]{2,1,0:T(8,128)S(1)} fusion(f32[48,64,1024]{2,0,1:T(8,128)} %all-gather.2.cloned.1.call-done, f32[8,16,64,1024]{3,2,1,0:T(8,128)} %param.7), kind=kOutput, calls=%fused_computation.3 | convolution fusion | flops 4831838208 | bytes 46161920 | tf_op jit(solution)/shard_map/dot_general | solution.py:15
  416.6 0.8 copy.47
  417.4 0.0 reduce-scatter.4.cloned.1.call-update
  417.4 0.1 broadcast_subtract_fusion
  417.5 53.7 %reduce-scatter.4.cloned.1.call-done = f32[8,16,3]{1,0,2:T(8,128)} async-done(((f32[8,16,48]{1,0,2:T(8,128)}), f32[8,16,3]{1,0,2:T(8,128)}) %reduce-scatter.4.cloned.1.call-update) | async-done | bytes 1552
  471.2 0.8 copy.48
  471.9 0.7 reshape.46
  472.6 3.2 all-to-all-start.1
  475.8 0.2 select_reduce_fusion
  476.0 3.6 all-to-all-done.1
  479.6 0.5 broadcast.40
  480.1 0.7 reduce
  480.8 0.1 reshape.47
  480.9 0.1 all_to_all.33
  481.0 1.4 fusion.8
  (6 shorter events, 0.0 us)
Async XLA Ops:
  6.5 359.7 %all-gather.2.cloned.1.call-start = ((), (), s32[]{:S(2)}) async-start(), calls=%async_computation.3 | async-start | bytes 18874368 | tf_op jit(solution)/shard_map/all_gather | solution.py:31
  206.2 6.4 %copy-start.3 = (s32[16]{0:T(128)S(1)}, s32[16]{0:T(128)}, u32[]{:S(2)}) copy-start(s32[16]{0:T(128)} %param.9) | copy-start | bytes 196
  206.2 6.5 %copy-start.2 = (s32[3,2]{0,1:T(2,128)S(1)}, s32[3,2]{0,1:T(2,128)}, u32[]{:S(2)}) copy-start(s32[3,2]{0,1:T(2,128)} %param.8) | copy-start | bytes 76
  206.2 6.5 %copy-start.1 = (f32[200]{0:T(256)S(1)}, f32[200]{0:T(256)}, u32[]{:S(2)}) copy-start(f32[200]{0:T(256)} %param.10) | copy-start | bytes 2404
  206.2 6.7 %copy-start = (f32[1024]{0:T(1024)S(1)}, f32[1024]{0:T(1024)}, u32[]{:S(2)}) copy-start(f32[1024]{0:T(1024)} %param.11) | copy-start | bytes 12292
  212.5 258.6 %reduce-scatter.4.cloned.1.call-start = ((), (), s32[]{:S(2)}) async-start(), calls=%async_computation.4 | async-start | bytes 208896
  472.6 7.0 %all-to-all-start.1 = ((f32[2,1,192]{2,1,0:T(1,128)}), f32[2,1,192]{2,1,0:T(1,128)S(1)}, u32[]{:S(2)}, u32[]{:S(2)}) async-start(f32[2,1,192]{2,1,0:T(1,128)} %reshape.46), calls=%async_computation.1 | async-start | bytes 4096 | tf_op jit(solution)/shard_map/all_to_all | solution.py:35
Sparse Core Ops, SparseCore 0:
  212.7 153.5 all-gather.1
  417.5 53.5 reduce-scatter.3
where the time goes:
time: 490 us; the launch traced here: 489 us
  waiting for transfers between devices  210 us (43%)
  blocking collectives  189 us (39%)
  matrix products  50.3 us (10%)
  local copies, waits for them, and re-layouts  19.7 us (4%)
  between operations  13.5 us (3%)
    all_to_all x1, blocking collectives, shards(): lax.all_to_all(amplitudes, 'wide', split_axis=1, concat_axis=0, tiled=True)  189 us
    all_gather x1, waiting for transfers between devices, shards(): lax.all_gather(exchanged, 'narrow', axis=2, tiled=True)  153 us
    unnamed x3, waiting for transfers between devices  53.7 us
    dot_general x1, matrix products, contract(): lax.dot_general(left_rows.reshape(left_rows.shape[0], -1), right_rows.res...  50.3 us
  transfers between devices with their start and end apart: 3, of which 3 were waited for; matrix products, arithmetic and copies ran while one was open for 0% of the time, Pallas kernels for 0%

commit v1 on v0

--- a/solution.py
+++ b/solution.py
@@ -2,6 +2,21 @@
 import jax.numpy as jnp
 from jax import lax
 from jax.sharding import PartitionSpec as P
+from jax.lax import axis_index, ppermute, psum
+
+
+def _compute_digits(local_array, dim_no, x_in):
+    back = local_array.shape
+    met_up = local_array.reshape(*back[:dim_no], x_in, back[dim_no] // x_in, *back[dim_no + 1 :])
+    last = jnp.moveaxis(met_up, dim_no, 0)
+    return last
+
+
+def link_pairs_all(piece_in, which_dim):
+    inter = list(piece_in.shape[1:])
+    inter[which_dim] *= piece_in.shape[0]
+    clean = jnp.moveaxis(piece_in, 0, which_dim).reshape(inter)
+    return clean
 
 
 def lookup(table, indices):
@@ -22,7 +37,22 @@
 
 
 def shards(amplitudes, integrals, pair_index, window_virtuals, occ_energy, virt_energy):
-    exchanged = lax.all_to_all(amplitudes, "wide", split_axis=1, concat_axis=0, tiled=True)
+
+    def step_on_racks_in(field_in, along_axis, slab_in, shard_in):
+        earlier = psum(1, axis_name=along_axis)
+        e_next, local_part = (earlier, axis_index(along_axis))
+        outer = _compute_digits(field_in, slab_in, e_next)
+        newest = outer
+        for u in range(1, e_next):
+            k_now, block_now = ((local_part + u) % e_next, (local_part - u) % e_next)
+            r2 = lax.dynamic_index_in_dim(outer, k_now, 0)
+            step_out = tuple(((w, (w + u) % e_next) for w in range(e_next)))
+            opened = ppermute(r2, axis_name=along_axis, perm=step_out)
+            newest = lax.dynamic_update_slice_in_dim(newest, opened, block_now, axis=0)
+        big = link_pairs_all(newest, shard_in)
+        return big
+
+    exchanged = step_on_racks_in(amplitudes, "wide", 1, 0)
     rows_here = integrals.shape[0]
     window = integrals.shape[1]
     first_block = integrals.shape[2]

time: 490 us -> 457 us (0.933)
  blocking collectives: 189 us -> 0 us
  starting transfers between devices: 3.26 us -> 72.8 us
  local copies, waits for them, and re-layouts: 19.7 us -> 86.9 us
  waiting for transfers between devices: 210 us -> 242 us
  matrix products: 50.3 us -> 39.2 us
    all_to_all x1 -> x0, blocking collectives: 189 us -> none  [shards(): lax.all_to_all(amplitudes, 'wide', split_axis=1, concat_axis=0, tiled=True)]
    ppermute x0 -> x15, starting transfers between devices: none -> 69.4 us  [step_on_racks_in(): opened = ppermute(r2, axis_name=along_axis, perm=step_out)]
    ppermute x0 -> x15, waiting for transfers between devices: none -> 63.2 us  [step_on_racks_in(): opened = ppermute(r2, axis_name=along_axis, perm=step_out)]
    unnamed x11 -> x13, local copies, waits for them, and re-layouts: 7.9 us -> 56.5 us
    all_gather x1, waiting for transfers between devices: 153 us -> 121 us  [shards(): lax.all_gather(exchanged, 'narrow', axis=2, tiled=True)]
    dynamic_update_slice x0 -> x16, local copies, waits for them, and re-layouts: none -> 23.3 us  [step_on_racks_in(): newest = lax.dynamic_update_slice_in_dim(newest, opened, block_now, axis=0)]
    dot_general x1, matrix products: 50.3 us -> 39.2 us  [contract(): lax.dot_general(left_rows.reshape(left_rows.shape[0], -1), right_rows.res...]
    all_to_all x3 -> x0, local copies, waits for them, and re-layouts: 9.52 us -> none  [shards(): lax.all_to_all(amplitudes, 'wide', split_axis=1, concat_axis=0, tiled=True)]
  transfers between devices with their start and end apart: 3 -> 18, of which waited for: 3 -> 7; matrix products, arithmetic and copies ran while one was open for 0% -> 11% of each run, Pallas kernels for 0% -> 0%
where the time goes in v1:
time: 457 us
  waiting for transfers between devices  242 us (53%)
  local copies, waits for them, and re-layouts  86.9 us (19%)
  starting transfers between devices  72.8 us (16%)
  matrix products  39.2 us (9%)
  between operations  13.5 us (3%)
    all_gather x1, waiting for transfers between devices, shards(): lax.all_gather(exchanged, 'narrow', axis=2, tiled=True)  121 us
    ppermute x15, starting transfers between devices, step_on_racks_in(): opened = ppermute(r2, axis_name=along_axis, perm=step_out)  69.4 us
    ppermute x15, waiting for transfers between devices, step_on_racks_in(): opened = ppermute(r2, axis_name=along_axis, perm=step_out)  63.2 us
    unnamed x13, local copies, waits for them, and re-layouts  56.5 us
    unnamed x3, waiting for transfers between devices  53.7 us
    dot_general x1, matrix products, contract(): lax.dot_general(left_rows.reshape(left_rows.shape[0], -1), right_rows.res...  39.2 us
    dynamic_update_slice x16, local copies, waits for them, and re-layouts, step_on_racks_in(): newest = lax.dynamic_update_slice_in_dim(newest, opened, block_now, axis=0)  23.3 us
  transfers between devices with their start and end apart: 18, of which 7 were waited for; matrix products, arithmetic and copies ran while one was open for 11% of the time, Pallas kernels for 0%

profile of v1, /device:TPU:0, one launch (start us, length us, event | category | flops | bytes accessed | tf_op | source)
XLA Modules:
  0.0 456.7 jit_solution(13121294733640293098)
XLA Ops:
  6.5 6.1 %copy.45 = f32[3,1024,512]{2,1,0:T(8,128)} copy(f32[3,1024,512]{2,1,0:T(8,128)} %param.6) | data formatting | bytes 12582912
  12.7 4.7 %dynamic-slice_bitcast_fusion = (f32[1,3,64,512]{3,2,0,1:T(8,128)S(1)}, f32[1,3,64,512]{3,2,0,1:T(8,128)S(1)}, f32[1,3,64,512]{3,2,0,1:T(8,128)S(1)}, f32[1,3,64...) fusion(f32[3,16,64,512]{3,2,1,0:T(8,128)} %bitcast.63, ...), kind=kLoop, calls=%fused_computation.1 | loop fusion | bytes 11796540 | tf_op jit(solution)/shard_map/jit(dynamic_index_in_dim)/dynamic_slice | solution.py:48
  17.8 2.5 collective-permute-start.1
  20.4 2.4 collective-permute-start.2
  22.8 1.6 collective-permute-start.3
  24.5 7.4 %collective-permute-done = f32[1,3,64,512]{3,2,0,1:T(8,128)} collective-permute-done((f32[1,3,64,512]{3,2,0,1:T(8,128)}, f32[1,3,64,512]{3,2,0,1:T(8,128)}, u32[]{:S(2)}, u32[]{:S(2)}) %collective-permute-start) | collective-permute-done | bytes 393248 | tf_op jit(solution)/shard_map/ppermute | solution.py:50
  32.5 1.8 constant_dynamic-update-slice_fusion.14
  34.2 7.3 %collective-permute-start.6 = (f32[1,3,64,512]{3,2,0,1:T(8,128)S(1)}, f32[1,3,64,512]{3,2,0,1:T(8,128)S(1)}, u32[]{:S(2)}, u32[]{:S(2)}) collective-permute-start(f32[1,3,64,512]{3,2,0,1:T(8,128)S(1)} %get-tuple-element.15), channel_id=1, source_target_pairs={{0,14},{2,16},{4,18},{6,20},{8,22},{10,24},{12,26},{14,28},{16,30}... | collective-permute-start | bytes 1179656 | tf_op jit(solution)/shard_map/ppermute | solution.py:50
  41.6 1.8 constant_dynamic-update-slice_fusion.13
  43.3 1.7 collective-permute-start.7
  45.0 1.8 constant_dynamic-update-slice_fusion.12
  46.8 1.8 constant_dynamic-update-slice_fusion.11
  48.6 51.5 %collective-permute-done.4 = f32[1,3,64,512]{3,2,0,1:T(8,128)} collective-permute-done((f32[1,3,64,512]{3,2,0,1:T(8,128)}, f32[1,3,64,512]{3,2,0,1:T(8,128)}, u32[]{:S(2)}, u32[]{:S(2)}) %collective-permute-start.4) | collective-permute-done | bytes 393248 | tf_op jit(solution)/shard_map/ppermute | solution.py:50
  100.1 1.8 constant_dynamic-update-slice_fusion.10
  101.9 10.0 %collective-permute-start.10 = (f32[1,3,64,512]{3,2,0,1:T(8,128)S(1)}, f32[1,3,64,512]{3,2,0,1:T(8,128)S(1)}, u32[]{:S(2)}, u32[]{:S(2)}) collective-permute-start(f32[1,3,64,512]{3,2,0,1:T(8,128)S(1)} %get-tuple-element.11), channel_id=1, source_target_pairs={{0,22},{2,24},{4,26},{6,28},{8,30},{10,0},{12,2},{14,4},{16,6},{18... | collective-permute-start | bytes 1179656 | tf_op jit(solution)/shard_map/ppermute | solution.py:50
  112.6 18.7 %collective-permute-start.11 = (f32[1,3,64,512]{3,2,0,1:T(8,128)S(1)}, f32[1,3,64,512]{3,2,0,1:T(8,128)S(1)}, u32[]{:S(2)}, u32[]{:S(2)}) collective-permute-start(f32[1,3,64,512]{3,2,0,1:T(8,128)S(1)} %get-tuple-element.10), channel_id=1, source_target_pairs={{0,24},{2,26},{4,28},{6,30},{8,0},{10,2},{12,4},{14,6},{16,8},{18,... | collective-permute-start | bytes 1179656 | tf_op jit(solution)/shard_map/ppermute | solution.py:50
  131.3 0.8 constant_dynamic-update-slice_fusion.8
  133.3 12.4 %collective-permute-start.13 = (f32[1,3,64,512]{3,2,0,1:T(8,128)S(1)}, f32[1,3,64,512]{3,2,0,1:T(8,128)S(1)}, u32[]{:S(2)}, u32[]{:S(2)}) collective-permute-start(f32[1,3,64,512]{3,2,0,1:T(8,128)S(1)} %get-tuple-element.8), channel_id=1, source_target_pairs={{0,28},{2,30},{4,0},{6,2},{8,4},{10,6},{12,8},{14,10},{16,12},{18,... | collective-permute-start | bytes 1179656 | tf_op jit(solution)/shard_map/ppermute | solution.py:50
  146.5 11.2 %collective-permute-start.14 = (f32[1,3,64,512]{3,2,0,1:T(8,128)S(1)}, f32[1,3,64,512]{3,2,0,1:T(8,128)S(1)}, u32[]{:S(2)}, u32[]{:S(2)}) collective-permute-start(f32[1,3,64,512]{3,2,0,1:T(8,128)S(1)} %get-tuple-element.7), channel_id=1, source_target_pairs={{0,30},{2,0},{4,2},{6,4},{8,6},{10,8},{12,10},{14,12},{16,14},{18,... | collective-permute-start | bytes 1179656 | tf_op jit(solution)/shard_map/ppermute | solution.py:50
  157.7 0.8 constant_dynamic-update-slice_fusion.5
  160.9 2.4 collective-permute-done.13
  164.0 1.8 collective-permute-done.14
  166.6 6.6 %copy.20 = f32[16,3,64,512]{3,2,1,0:T(8,128)} copy(f32[16,3,64,512]{3,2,0,1:T(8,128)} %constant_dynamic-update-slice_fusion) | data formatting | bytes 12582912 | tf_op jit(solution)/shard_map/dynamic_update_slice | solution.py:51
  173.6 33.1 %copy.26 = f32[16,8,64,1024]{3,1,2,0:T(8,128)} copy(f32[16,8,64,1024]{3,2,1,0:T(8,128)} %bitcast.65) | data formatting | bytes 67108864
  207.2 121.1 %all-gather.2.cloned.1.call-done = f32[48,64,1024]{2,1,0:T(8,128)} async-done(((f32[48,64,512]{2,1,0:T(8,128)}), f32[48,64,1024]{2,1,0:T(8,128)}) %all-gather.2.cloned.1.call-update) | async-done | bytes 12582928 | tf_op jit(solution)/shard_map/all_gather | solution.py:61
  328.3 16.5 %copy.25 = f32[6,8,64,1024]{3,1,2,0:T(8,128)} copy(f32[6,8,64,1024]{3,2,1,0:T(8,128)} %bitcast.67) | data formatting | bytes 25165824
  344.8 39.2 %convolution_bitcast_fusion = f32[128,48]{0,1:T(8,128)S(1)} fusion(f32[48,65536]{1,0:T(8,128)} %bitcast.62, f32[128,65536]{1,0:T(8,128)} %bitcast.61), kind=kOutput, calls=%fused_computation | convolution fusion | flops 4831838208 | bytes 46161920 | tf_op jit(solution)/shard_map/dot_general | solution.py:30
  384.0 0.8 copy.22
  384.9 53.7 %reduce-scatter.4.cloned.1.call-done = f32[8,16,3]{1,0,2:T(8,128)} async-done(((f32[8,16,48]{1,0,2:T(8,128)}), f32[8,16,3]{1,0,2:T(8,128)}) %reduce-scatter.4.cloned.1.call-update) | async-done | bytes 1552
  440.1 3.2 all-to-all-start
  443.5 3.6 all-to-all-done
  448.4 1.4 fusion
  (52 shorter events, 11.7 us)
Async XLA Ops:
  6.5 321.8 %all-gather.2.cloned.1.call-start = ((), (), s32[]{:S(2)}) async-start(), calls=%async_computation.2 | async-start | bytes 18874368 | tf_op jit(solution)/shard_map/all_gather | solution.py:61
  17.4 14.6 %collective-permute-start = (f32[1,3,64,512]{3,2,0,1:T(8,128)}, f32[1,3,64,512]{3,2,0,1:T(8,128)}, u32[]{:S(2)}, u32[]{:S(2)}) collective-permute-start(f32[1,3,64,512]{3,2,0,1:T(8,128)} %get-tuple-element.21), channel_id=1, source_target_pairs={{0,2},{2,4},{4,6},{6,8},{8,10},{10,12},{12,14},{14,16},{16,18},{18... | collective-permute-start | bytes 1179656 | tf_op jit(solution)/shard_map/ppermute | solution.py:50
  17.8 16.4 %collective-permute-start.1 = (f32[1,3,64,512]{3,2,0,1:T(8,128)}, f32[1,3,64,512]{3,2,0,1:T(8,128)}, u32[]{:S(2)}, u32[]{:S(2)}) collective-permute-start(f32[1,3,64,512]{3,2,0,1:T(8,128)} %get-tuple-element.20), channel_id=1, source_target_pairs={{0,4},{2,6},{4,8},{6,10},{8,12},{10,14},{12,16},{14,18},{16,20},{1... | collective-permute-start | bytes 1179656 | tf_op jit(solution)/shard_map/ppermute | solution.py:50
  20.4 23.0 %collective-permute-start.2 = (f32[1,3,64,512]{3,2,0,1:T(8,128)}, f32[1,3,64,512]{3,2,0,1:T(8,128)}, u32[]{:S(2)}, u32[]{:S(2)}) collective-permute-start(f32[1,3,64,512]{3,2,0,1:T(8,128)} %get-tuple-element.19), channel_id=1, source_target_pairs={{0,6},{2,8},{4,10},{6,12},{8,14},{10,16},{12,18},{14,20},{16,22},{... | collective-permute-start | bytes 1179656 | tf_op jit(solution)/shard_map/ppermute | solution.py:50
  22.8 24.0 %collective-permute-start.3 = (f32[1,3,64,512]{3,2,0,1:T(8,128)}, f32[1,3,64,512]{3,2,0,1:T(8,128)}, u32[]{:S(2)}, u32[]{:S(2)}) collective-permute-start(f32[1,3,64,512]{3,2,0,1:T(8,128)} %get-tuple-element.18), channel_id=1, source_target_pairs={{0,8},{2,10},{4,12},{6,14},{8,16},{10,18},{12,20},{14,22},{16,24},... | collective-permute-start | bytes 1179656 | tf_op jit(solution)/shard_map/ppermute | solution.py:50
  24.4 75.7 %collective-permute-start.4 = (f32[1,3,64,512]{3,2,0,1:T(8,128)}, f32[1,3,64,512]{3,2,0,1:T(8,128)}, u32[]{:S(2)}, u32[]{:S(2)}) collective-permute-start(f32[1,3,64,512]{3,2,0,1:T(8,128)} %get-tuple-element.17), channel_id=1, source_target_pairs={{0,10},{2,12},{4,14},{6,16},{8,18},{10,20},{12,22},{14,24},{16,26}... | collective-permute-start | bytes 1179656 | tf_op jit(solution)/shard_map/ppermute | solution.py:50
  32.0 69.9 %collective-permute-start.5 = (f32[1,3,64,512]{3,2,0,1:T(8,128)}, f32[1,3,64,512]{3,2,0,1:T(8,128)S(1)}, u32[]{:S(2)}, u32[]{:S(2)}) collective-permute-start(f32[1,3,64,512]{3,2,0,1:T(8,128)} %get-tuple-element.16), channel_id=1, source_target_pairs={{0,12},{2,14},{4,16},{6,18},{8,20},{10,22},{12,24},{14,26},{16,28}... | collective-permute-start | bytes 1179656 | tf_op jit(solution)/shard_map/ppermute | solution.py:50
  34.2 78.4 %collective-permute-start.6 = (f32[1,3,64,512]{3,2,0,1:T(8,128)S(1)}, f32[1,3,64,512]{3,2,0,1:T(8,128)S(1)}, u32[]{:S(2)}, u32[]{:S(2)}) collective-permute-start(f32[1,3,64,512]{3,2,0,1:T(8,128)S(1)} %get-tuple-element.15), channel_id=1, source_target_pairs={{0,14},{2,16},{4,18},{6,20},{8,22},{10,24},{12,26},{14,28},{16,30}... | collective-permute-start | bytes 1179656 | tf_op jit(solution)/shard_map/ppermute | solution.py:50
  43.3 88.8 %collective-permute-start.7 = (f32[1,3,64,512]{3,2,0,1:T(8,128)S(1)}, f32[1,3,64,512]{3,2,0,1:T(8,128)S(1)}, u32[]{:S(2)}, u32[]{:S(2)}) collective-permute-start(f32[1,3,64,512]{3,2,0,1:T(8,128)S(1)} %get-tuple-element.14), channel_id=1, source_target_pairs={{0,16},{2,18},{4,20},{6,22},{8,24},{10,26},{12,28},{14,30},{16,0},... | collective-permute-start | bytes 1179656 | tf_op jit(solution)/shard_map/ppermute | solution.py:50
  46.8 86.6 %collective-permute-start.8 = (f32[1,3,64,512]{3,2,0,1:T(8,128)S(1)}, f32[1,3,64,512]{3,2,0,1:T(8,128)S(1)}, u32[]{:S(2)}, u32[]{:S(2)}) collective-permute-start(f32[1,3,64,512]{3,2,0,1:T(8,128)S(1)} %get-tuple-element.13), channel_id=1, source_target_pairs={{0,18},{2,20},{4,22},{6,24},{8,26},{10,28},{12,30},{14,0},{16,2},{... | collective-permute-start | bytes 1179656 | tf_op jit(solution)/shard_map/ppermute | solution.py:50
  100.1 46.4 %collective-permute-start.9 = (f32[1,3,64,512]{3,2,0,1:T(8,128)S(1)}, f32[1,3,64,512]{3,2,0,1:T(8,128)S(1)}, u32[]{:S(2)}, u32[]{:S(2)}) collective-permute-start(f32[1,3,64,512]{3,2,0,1:T(8,128)S(1)} %get-tuple-element.12), channel_id=1, source_target_pairs={{0,20},{2,22},{4,24},{6,26},{8,28},{10,30},{12,0},{14,2},{16,4},{1... | collective-permute-start | bytes 1179656 | tf_op jit(solution)/shard_map/ppermute | solution.py:50
  101.9 56.7 %collective-permute-start.10 = (f32[1,3,64,512]{3,2,0,1:T(8,128)S(1)}, f32[1,3,64,512]{3,2,0,1:T(8,128)S(1)}, u32[]{:S(2)}, u32[]{:S(2)}) collective-permute-start(f32[1,3,64,512]{3,2,0,1:T(8,128)S(1)} %get-tuple-element.11), channel_id=1, source_target_pairs={{0,22},{2,24},{4,26},{6,28},{8,30},{10,0},{12,2},{14,4},{16,6},{18... | collective-permute-start | bytes 1179656 | tf_op jit(solution)/shard_map/ppermute | solution.py:50
  112.6 46.7 %collective-permute-start.11 = (f32[1,3,64,512]{3,2,0,1:T(8,128)S(1)}, f32[1,3,64,512]{3,2,0,1:T(8,128)S(1)}, u32[]{:S(2)}, u32[]{:S(2)}) collective-permute-start(f32[1,3,64,512]{3,2,0,1:T(8,128)S(1)} %get-tuple-element.10), channel_id=1, source_target_pairs={{0,24},{2,26},{4,28},{6,30},{8,0},{10,2},{12,4},{14,6},{16,8},{18,... | collective-permute-start | bytes 1179656 | tf_op jit(solution)/shard_map/ppermute | solution.py:50
  132.1 28.0 %collective-permute-start.12 = (f32[1,3,64,512]{3,2,0,1:T(8,128)S(1)}, f32[1,3,64,512]{3,2,0,1:T(8,128)S(1)}, u32[]{:S(2)}, u32[]{:S(2)}) collective-permute-start(f32[1,3,64,512]{3,2,0,1:T(8,128)S(1)} %get-tuple-element.9), channel_id=1, source_target_pairs={{0,26},{2,28},{4,30},{6,0},{8,2},{10,4},{12,6},{14,8},{16,10},{18,... | collective-permute-start | bytes 1179656 | tf_op jit(solution)/shard_map/ppermute | solution.py:50
  133.3 29.9 %collective-permute-start.13 = (f32[1,3,64,512]{3,2,0,1:T(8,128)S(1)}, f32[1,3,64,512]{3,2,0,1:T(8,128)S(1)}, u32[]{:S(2)}, u32[]{:S(2)}) collective-permute-start(f32[1,3,64,512]{3,2,0,1:T(8,128)S(1)} %get-tuple-element.8), channel_id=1, source_target_pairs={{0,28},{2,30},{4,0},{6,2},{8,4},{10,6},{12,8},{14,10},{16,12},{18,... | collective-permute-start | bytes 1179656 | tf_op jit(solution)/shard_map/ppermute | solution.py:50
  146.5 19.3 %collective-permute-start.14 = (f32[1,3,64,512]{3,2,0,1:T(8,128)S(1)}, f32[1,3,64,512]{3,2,0,1:T(8,128)S(1)}, u32[]{:S(2)}, u32[]{:S(2)}) collective-permute-start(f32[1,3,64,512]{3,2,0,1:T(8,128)S(1)} %get-tuple-element.7), channel_id=1, source_target_pairs={{0,30},{2,0},{4,2},{6,4},{8,6},{10,8},{12,10},{14,12},{16,14},{18,... | collective-permute-start | bytes 1179656 | tf_op jit(solution)/shard_map/ppermute | solution.py:50
  173.3 265.3 %reduce-scatter.4.cloned.1.call-start = ((), (), s32[]{:S(2)}) async-start(), calls=%async_computation.3 | async-start | bytes 208896
  173.5 33.2 %copy-start.3 = (s32[16]{0:T(128)S(1)}, s32[16]{0:T(128)}, u32[]{:S(2)}) copy-start(s32[16]{0:T(128)} %param.9) | copy-start | bytes 196
  173.5 33.3 %copy-start.2 = (s32[3,2]{0,1:T(2,128)S(1)}, s32[3,2]{0,1:T(2,128)}, u32[]{:S(2)}) copy-start(s32[3,2]{0,1:T(2,128)} %param.8) | copy-start | bytes 76
  173.5 33.3 %copy-start.1 = (f32[200]{0:T(256)S(1)}, f32[200]{0:T(256)}, u32[]{:S(2)}) copy-start(f32[200]{0:T(256)} %param.10) | copy-start | bytes 2404
  173.5 33.5 %copy-start = (f32[1024]{0:T(1024)S(1)}, f32[1024]{0:T(1024)}, u32[]{:S(2)}) copy-start(f32[1024]{0:T(1024)} %param.11) | copy-start | bytes 12292
  440.1 7.0 %all-to-all-start = ((f32[2,1,192]{2,1,0:T(1,128)}), f32[2,1,192]{2,1,0:T(1,128)S(1)}, u32[]{:S(2)}, u32[]{:S(2)}) async-start(f32[2,1,192]{2,1,0:T(1,128)} %reshape.71), calls=%async_computation | async-start | bytes 4096 | tf_op jit(solution)/shard_map/all_to_all | solution.py:65
Sparse Core Ops, SparseCore 0:
  173.4 154.8 all-gather.1
  385.0 53.5 reduce-scatter.3
